TPU v7x, 32 devices: a whole 2x2x4 slice. The times are simulated.
32 devices in a mesh: parts: 2 (over y), req: 4 (over z), tp: 2 (over x), sp: 2 (over core).
Axes of the slice: x: 2, y: 2, z: 4, core: 2. Of those that a mesh axis runs over, the one named last changes fastest.
Arguments:
- prompt_x: bfloat16 [1024, 16384], P(('parts', 'req', 'sp'), 'tp'), parts along dimension 0, may hold values from -600 to 600
- prompt_b: bfloat16 [1024, 8, 128], P(('parts', 'req', 'sp'), 'tp'), parts along dimension 0, may hold values from -0.5 to 0.5
- prompt_dt: float32 [1024, 256], P(('parts', 'req', 'sp'), 'tp'), parts along dimension 0, may hold values from 0.5 to 2
- cont_x: bfloat16 [8, 256, 16384], P(('parts', 'req'), 'sp', 'tp'), parts along dimension 0, may hold values from -6 to 6
- cont_bc: bfloat16 [8, 256, 2, 8, 128], P(('parts', 'req'), 'sp', None, 'tp'), parts along dimension 0, may hold values from -0.5 to 0.5
- cont_dt: float32 [8, 256, 256], P(('parts', 'req'), 'sp', 'tp'), parts along dimension 0, may hold values from 0.5 to 2
- decay_rate: float32 [256], P('tp'), may hold values from 0.0063476562 to 0.05
- skip_gain: float32 [256], P('tp'), may hold values from 0.5 to 1.5
- norm_gain: float32 [16384], P('tp'), may hold values from 0.25 to 1.75
- steer_vecs: float32 [7, 16384], P(None, 'tp'), may hold values from -3 to 3
- mult_table: float32 [9], replicated, may hold values from -3 to 3
- mult_idx: int32 [8], P(('parts', 'req')), parts along dimension 0, may hold values from 0 to 8
- behav_idx: int32 [8], P(('parts', 'req')), parts along dimension 0, may hold values from 0 to 6
Outputs:
- steered_out: bfloat16 [8, 256, 16384], P(('parts', 'req'), 'sp', 'tp'), parts along dimension 0
There are 2 independent parts, one for each index of `parts`. A program takes and returns all parts, laid end to end along the dimension named above; an argument that names none is the same for every part. Nothing has to cross between parts.
All inputs are finite; a program needn't handle non-finite values.
Results may differ from a plain program's by a relative error of at most 0.008.
Values sent between devices are 32-bit elements; how exact they have to be, the bound alone decides.
A program may use at most 320 MiB of HBM per device.

v0:
```python
import jax
import jax.numpy as jnp
from jax import lax
from jax.sharding import PartitionSpec as P

HEADS = 256
HEAD_DIM = 64


def carried_in(array, axis, combine, identity):
    peers, mine = (lax.axis_size(axis), lax.axis_index(axis))
    everything = jax.tree.map(lambda part: lax.all_gather(part, axis), array)
    start = jax.tree.map(
        lambda part, zero: jnp.broadcast_to(jnp.asarray(zero, part.dtype), part.shape),
        array,
        identity,
    )

    def turn(k, before):
        reached = k < mine
        new = combine(before, jax.tree.map(lambda part: part[k], everything))
        return jax.tree.map(lambda a, b: jnp.where(reached, a, b), new, before)

    return lax.fori_loop(0, peers, turn, start)


def spread(array, axis, root):
    mine = lax.axis_index(axis) == root
    return lax.psum(jnp.where(mine, array, jnp.zeros_like(array)), axis)


def block_state(rows_x, rows_b, rows_dt, decay_rate, groups):
    length = rows_x.shape[0]
    head_count = decay_rate.shape[0]
    per_group = head_count // groups
    head_size = rows_x.shape[1] // head_count
    cumulative = jnp.cumsum(-decay_rate[None, :] * rows_dt, axis=0)
    block_total = cumulative[-1]
    weight = jnp.exp(block_total[None, :] - cumulative) * rows_dt
    scaled = (
        rows_x.astype(jnp.float32).reshape(length, head_count, head_size) * weight[:, :, None]
    ).astype(jnp.bfloat16)
    scaled = scaled.reshape(length, groups, per_group, head_size)
    local_state = jnp.einsum("tgqp,tgn->gqpn", scaled, rows_b, preferred_element_type=jnp.float32)
    carried = jnp.einsum(
        "tgq,tgn->gqn",
        weight.reshape(length, groups, per_group),
        rows_b.astype(jnp.float32),
        precision=lax.Precision.HIGHEST,
    )
    return (
        block_total,
        local_state.reshape(head_count, head_size, -1),
        carried.reshape(head_count, -1),
        cumulative,
    )


def intra_block(steered, bmat, cmat, rows_dt, cumulative, groups):
    length = steered.shape[0]
    head_count = rows_dt.shape[1]
    per_group = head_count // groups
    head_size = steered.shape[1] // head_count
    products = jnp.einsum("tgn,sgn->gts", cmat, bmat, preferred_element_type=jnp.float32)
    lower_mask = lax.broadcasted_iota(jnp.int32, (length, length), 0) >= lax.broadcasted_iota(
        jnp.int32, (length, length), 1
    )
    row_factor = jnp.exp(cumulative).reshape(length, groups, per_group).transpose(1, 2, 0)
    col_factor = (
        (jnp.exp(-cumulative) * rows_dt).reshape(length, groups, per_group).transpose(1, 2, 0)
    )
    full = products[:, None, :, :] * row_factor[:, :, :, None] * col_factor[:, :, None, :]
    mixing = jnp.where(lower_mask[None, None], full, 0.0).astype(jnp.bfloat16)
    input_groups = steered.reshape(length, groups, per_group, head_size)
    outputs = jnp.einsum(
        "gqts,sgqp->tgqp", mixing, input_groups, preferred_element_type=jnp.float32
    )
    return outputs.reshape(length, head_count, head_size)


def chain_link(earlier, later):
    decay_all = jnp.exp(later[0])
    return (
        earlier[0] + later[0],
        decay_all[:, None, None] * earlier[1] + later[1],
        decay_all[:, None] * earlier[2] + later[2],
    )


def link_blocks(earlier, later):
    return (earlier[0] + later[0], jnp.exp(later[0])[:, None, None] * earlier[1] + later[1])


def local(
    prompt_x,
    prompt_b,
    prompt_dt,
    cont_x,
    cont_bc,
    cont_dt,
    decay_rate,
    skip_gain,
    norm_gain,
    steer_vecs,
    mult_table,
    mult_idx,
    behav_idx,
):
    groups = prompt_b.shape[1]
    head_count = decay_rate.shape[0]
    per_group = head_count // groups
    head_size = norm_gain.shape[0] // head_count
    prompt_total, prompt_state, prompt_carry, unused = block_state(
        prompt_x, prompt_b, prompt_dt, decay_rate, groups
    )
    identity = (
        jnp.zeros_like(prompt_total),
        jnp.zeros_like(prompt_state),
        jnp.zeros_like(prompt_carry),
    )
    before = carried_in(
        (prompt_total, prompt_state, prompt_carry), ("req", "sp"), chain_link, identity
    )
    inclusive = chain_link(before, (prompt_total, prompt_state, prompt_carry))
    prefix_state, prefix_carry = (
        spread(inclusive[1], ("req", "sp"), lax.axis_size(("req", "sp")) - 1),
        spread(inclusive[2], ("req", "sp"), lax.axis_size(("req", "sp")) - 1),
    )
    picked = lax.broadcasted_iota(jnp.int32, mult_table.shape, 0) == mult_idx[0]
    multiplier = jnp.sum(jnp.where(picked, mult_table, 0.0))
    choose = lax.broadcasted_iota(jnp.int32, (steer_vecs.shape[0], 1), 0) == behav_idx[0]
    vector = jnp.sum(jnp.where(choose, steer_vecs, 0.0), axis=0)
    steered = (cont_x[0].astype(jnp.float32) + multiplier * vector[None, :]).astype(jnp.bfloat16)
    bmat = cont_bc[0, :, 0]
    cmat = cont_bc[0, :, 1]
    rows_dt = cont_dt[0]
    length = steered.shape[0]
    block_total, local_state, carried, cumulative = block_state(
        steered, bmat, rows_dt, decay_rate, groups
    )
    before_total, before_state = carried_in(
        (block_total, local_state),
        "sp",
        link_blocks,
        (jnp.zeros_like(block_total), jnp.zeros_like(local_state)),
    )
    inner = intra_block(steered, bmat, cmat, rows_dt, cumulative, groups)
    start_state = (
        prefix_state
        + multiplier * vector.reshape(head_count, head_size)[:, :, None] * prefix_carry[:, None, :]
    )
    incoming = jnp.exp(before_total)[:, None, None] * start_state + before_state
    incoming_round = incoming.astype(jnp.bfloat16).reshape(groups, per_group, head_size, -1)
    from_state = jnp.einsum(
        "tgn,gqpn->tgqp", cmat, incoming_round, preferred_element_type=jnp.float32
    ).reshape(length, head_count, head_size)
    skipped = skip_gain[None, :, None] * steered.astype(jnp.float32).reshape(
        length, head_count, head_size
    )
    mixed = (inner + jnp.exp(cumulative)[:, :, None] * from_state + skipped).reshape(
        length, head_count * head_size
    )
    squares = jnp.sum(mixed * mixed, axis=1)
    total_squares = lax.psum(squares, "tp")
    meansq = total_squares / (HEADS * HEAD_DIM)
    return (mixed * lax.rsqrt(meansq + 1e-05)[:, None] * norm_gain[None, :]).astype(jnp.bfloat16)[
        None
    ]


def solution(mesh):
    return jax.shard_map(
        local,
        mesh=mesh,
        in_specs=(
            P(("parts", "req", "sp"), "tp"),
            P(("parts", "req", "sp"), "tp", None),
            P(("parts", "req", "sp"), "tp"),
            P(("parts", "req"), "sp", "tp"),
            P(("parts", "req"), "sp", None, "tp", None),
            P(("parts", "req"), "sp", "tp"),
            P("tp"),
            P("tp"),
            P("tp"),
            P(None, "tp"),
            P(),
            P(("parts", "req")),
            P(("parts", "req")),
        ),
        out_specs=P(("parts", "req"), "sp", "tp"),
        check_vma=False,
    )
```

profile of v0, /device:TPU:0, one launch (start us, length us, event | category | flops | bytes accessed | tf_op | source)
XLA Modules:
  0.0 499.8 jit_solution(6376185409903289306)
XLA Ops:
  7.2 0.8 broadcast_multiply_fusion
  8.7 0.8 exponential_multiply_fusion.1
  9.5 3.3 copy.53
  12.9 4.9 fusion.22
  17.9 0.8 copy-done.5
  21.9 3.2 copy.39
  25.4 2.9 fusion.23
  28.8 1.9 all-gather
  30.8 13.3 %all-gather.1 = f32[8,1,128]{2,1,0:T(1,128)S(1)} all-gather(f32[1,1,128]{2,1,0:T(1,128)S(1)} %copy-done.9), channel_id=1, replica_groups=mesh['parts'=2,'req'=4,'tp'=2,'sp'=2] {'req','sp'}, dimensions={0}, use_global_device_ids=true | all-gather | bytes 4608 | tf_op jit(solution)/shard_map/all_gather | solution.py:12
  44.9 22.9 %all_gather.19 = f32[8,128,128]{2,1,0:T(8,128)S(1)} all-gather(f32[1,128,128]{2,1,0:T(8,128)S(1)} %bitcast.124), channel_id=1, replica_groups=mesh['parts'=2,'req'=4,'tp'=2,'sp'=2] {'req','sp'}, dimensions={0}, use_global_device_ids=true | all-gather | bytes 589824 | tf_op jit(solution)/shard_map/all_gather | solution.py:12
  67.7 245.8 %all-gather.7.cloned.1.call-done = f32[8,128,64,128]{3,2,1,0:T(8,128)} async-done(((f32[1,128,64,128]{3,2,1,0:T(8,128)}), f32[8,128,64,128]{3,2,1,0:T(8,128)}) %all-gather.7.cloned.1.call-update) | async-done | bytes 33554448 | tf_op jit(solution)/shard_map/all_gather | solution.py:12
  313.6 50.9 %while.33 = (s32[]{:T(128)}, f32[128,64,128]{2,1,0:T(8,128)}, f32[128,128]{1,0:T(8,128)S(1)}, s32[]{:T(128)}, f32[8,128]{1,0:T(8,128)S(1)}, /*index=5*/f32[8,128...) while((s32[]{:T(128)}, f32[128,64,128]{2,1,0:T(8,128)}, ...), condition=%wide.region_7.8_spmd.clone, body=%wide.region_6.7_spmd.clone.sunk | while | flops 4259844 | bytes 12781695 | solution.py:24
  313.6 4.8 fusion.54
  318.5 7.6 %fusion.54 = f32[128,64,128]{2,1,0:T(8,128)} fusion(f32[8,128,64,128]{3,2,1,0:T(8,128)} %get-tuple-element.464, s32[]{:T(128)} %get-tuple-element.450, f32[128,64,128]{2,1,0:T(8,128)} %get-tuple-element.451, f32[128]{0:T(128)S(1)} %fusion.53, pred[]{:T(512)S(6)} %compare.7, pred[]{:T(512)S(6)} %lt.46), kind=kLoop, calls=%fused_computation.7.clone.1 | loop fusion | flops 4194304 | bytes 12583430 | tf_op jit(solution)/shard_map/while/body/eval_jaxpr/jit(_where)/select_n | solution.py:22
  326.2 7.3 %fusion.54 = f32[128,64,128]{2,1,0:T(8,128)} fusion(f32[8,128,64,128]{3,2,1,0:T(8,128)} %get-tuple-element.464, s32[]{:T(128)} %get-tuple-element.450, f32[128,64,128]{2,1,0:T(8,128)} %get-tuple-element.451, f32[128]{0:T(128)S(1)} %fusion.53, pred[]{:T(512)S(6)} %compare.7, pred[]{:T(512)S(6)} %lt.46), kind=kLoop, calls=%fused_computation.7.clone.1 | loop fusion | flops 4194304 | bytes 12583430 | tf_op jit(solution)/shard_map/while/body/eval_jaxpr/jit(_where)/select_n | solution.py:22
  333.6 6.0 %fusion.54 = f32[128,64,128]{2,1,0:T(8,128)} fusion(f32[8,128,64,128]{3,2,1,0:T(8,128)} %get-tuple-element.464, s32[]{:T(128)} %get-tuple-element.450, f32[128,64,128]{2,1,0:T(8,128)} %get-tuple-element.451, f32[128]{0:T(128)S(1)} %fusion.53, pred[]{:T(512)S(6)} %compare.7, pred[]{:T(512)S(6)} %lt.46), kind=kLoop, calls=%fused_computation.7.clone.1 | loop fusion | flops 4194304 | bytes 12583430 | tf_op jit(solution)/shard_map/while/body/eval_jaxpr/jit(_where)/select_n | solution.py:22
  339.8 6.0 %fusion.54 = f32[128,64,128]{2,1,0:T(8,128)} fusion(f32[8,128,64,128]{3,2,1,0:T(8,128)} %get-tuple-element.464, s32[]{:T(128)} %get-tuple-element.450, f32[128,64,128]{2,1,0:T(8,128)} %get-tuple-element.451, f32[128]{0:T(128)S(1)} %fusion.53, pred[]{:T(512)S(6)} %compare.7, pred[]{:T(512)S(6)} %lt.46), kind=kLoop, calls=%fused_computation.7.clone.1 | loop fusion | flops 4194304 | bytes 12583430 | tf_op jit(solution)/shard_map/while/body/eval_jaxpr/jit(_where)/select_n | solution.py:22
  346.0 6.0 %fusion.54 = f32[128,64,128]{2,1,0:T(8,128)} fusion(f32[8,128,64,128]{3,2,1,0:T(8,128)} %get-tuple-element.464, s32[]{:T(128)} %get-tuple-element.450, f32[128,64,128]{2,1,0:T(8,128)} %get-tuple-element.451, f32[128]{0:T(128)S(1)} %fusion.53, pred[]{:T(512)S(6)} %compare.7, pred[]{:T(512)S(6)} %lt.46), kind=kLoop, calls=%fused_computation.7.clone.1 | loop fusion | flops 4194304 | bytes 12583430 | tf_op jit(solution)/shard_map/while/body/eval_jaxpr/jit(_where)/select_n | solution.py:22
  352.2 6.0 %fusion.54 = f32[128,64,128]{2,1,0:T(8,128)} fusion(f32[8,128,64,128]{3,2,1,0:T(8,128)} %get-tuple-element.464, s32[]{:T(128)} %get-tuple-element.450, f32[128,64,128]{2,1,0:T(8,128)} %get-tuple-element.451, f32[128]{0:T(128)S(1)} %fusion.53, pred[]{:T(512)S(6)} %compare.7, pred[]{:T(512)S(6)} %lt.46), kind=kLoop, calls=%fused_computation.7.clone.1 | loop fusion | flops 4194304 | bytes 12583430 | tf_op jit(solution)/shard_map/while/body/eval_jaxpr/jit(_where)/select_n | solution.py:22
  358.3 6.0 %fusion.54 = f32[128,64,128]{2,1,0:T(8,128)} fusion(f32[8,128,64,128]{3,2,1,0:T(8,128)} %get-tuple-element.464, s32[]{:T(128)} %get-tuple-element.450, f32[128,64,128]{2,1,0:T(8,128)} %get-tuple-element.451, f32[128]{0:T(128)S(1)} %fusion.53, pred[]{:T(512)S(6)} %compare.7, pred[]{:T(512)S(6)} %lt.46), kind=kLoop, calls=%fused_computation.7.clone.1 | loop fusion | flops 4194304 | bytes 12583430 | tf_op jit(solution)/shard_map/while/body/eval_jaxpr/jit(_where)/select_n | solution.py:22
  364.5 0.7 fusion.37
  365.2 5.9 %fusion.11 = f32[128,64,128]{2,1,0:T(8,128)} fusion(f32[4,32,64,128]{3,2,1,0:T(8,128)} %fusion.22, f32[128,64,128]{2,1,0:T(8,128)} %get-tuple-element.241, f32[128]{0:T(128)S(1)} %copy-done.7, pred[]{:T(512)S(6)} %eq.25), kind=kLoop, calls=%fused_computation.24 | loop fusion | flops 3145728 | bytes 12583425 | tf_op jit(solution)/shard_map/jit(_where)/select_n | solution.py:29
  371.4 6.3 %fusion.9 = f32[4,32,64,128]{3,2,1,0:T(8,128)} fusion(f32[4,32,128]{2,1,0:T(8,128)S(1)} %get-tuple-element.325, f32[4,32,128]{2,1,0:T(8,128)S(1)} %get-tuple-element.324, f32[4,128,128]{2,1,0:T(8,128)S(1)} %fusion.30, pred[128,128]{1,0:T(8,128)(4,1)S(1)} %iota_compare_fusion, f32[4,32,64]{2,1,0:T(8,128)S(1)} %mul.272, bf16[128,4,32,64]{0,3,2,1:T(8,128)(2,1)S(1)} %bitcast.115), kind=kOutput, calls=%fused_computation.20 | convolution fusion | flops 279969792 | bytes 6733824 | tf_op jit(solution)/shard_map/gqts,sgqp->tgqp/dot_general | solution.py:75
  377.7 10.9 %while.32 = (s32[]{:T(128)}, f32[128]{0:T(128)S(1)}, f32[128,64,128]{2,1,0:T(8,128)}, s32[]{:T(128)}, f32[2,128]{1,0:T(2,128)S(1)}, /*index=5*/f32[2,128,64,128]{3,2,1,0:T(8,128)}, s32[]{:T(128)}, s32[]{:T(128)}) while((s32[]{:T(128)}, f32[128]{0:T(128)S(1)}, f32[128,64,128]{2,1,0:T(8,128)}, s32[]{:T(128)}, ...), condition=%wide.region_4.5_spmd.clone, body=%wide.region_3.4_spmd.clone.sunk | while | flops 4194692 | bytes 12585587 | solution.py:24
  377.7 4.7 fusion.52
  382.4 6.1 %fusion.52 = f32[128,64,128]{2,1,0:T(8,128)} fusion(f32[2,128,64,128]{3,2,1,0:T(8,128)} %get-tuple-element.438, s32[]{:T(128)} %get-tuple-element.425, f32[128,64,128]{2,1,0:T(8,128)} %get-tuple-element.427, f32[128]{0:T(128)S(1)} %get-tuple-element.409, pred[]{:T(512)S(6)} %compare.6, pred[]{:T(512)S(6)} %lt.45), kind=kLoop, calls=%fused_computation.1.clone.1 | loop fusion | flops 4194304 | bytes 12583430 | tf_op jit(solution)/shard_map/while/body/eval_jaxpr/jit(_where)/select_n | solution.py:22
  388.5 79.2 %all-reduce.3.cloned.1.call-done = (f32[128,64,128]{2,1,0:T(8,128)}, f32[128,128]{1,0:T(8,128)}) async-done(((f32[128,64,128]{2,1,0:T(8,128)}, f32[128,128]{1,0:T(8,128)}), (f32[128,64,128]{2,1,0:T(8,128)}, f32[128,128]{1,0:T(8,128)})) %all-reduce.3.cloned.1.call-update) | async-done | bytes 4259856 | tf_op jit(solution)/shard_map/psum | solution.py:29
  467.8 4.4 add_convert_fusion.1
  472.4 3.3 fusion.8
  475.7 4.9 psum.23
  480.6 8.6 %fusion.16 = bf16[1,128,8192]{1,2,0:T(8,128)(2,1)} fusion(f32[1,128,8192]{1,2,0:T(8,128)} %bitcast.119, f32[1,128,8192]{1,2,0:T(8,128)} %bitcast.120, f32[8192]{0:T(1024)S(1)} %copy-done.6, f32[128]{0:T(128)S(1)} %add_rsqrt_fusion, f32[8192]{0:T(1024)S(1)} %broadcast_multiply_fusion.1, f32[8192]{0:T(1024)S(1)} %mul.305, f32[128,128]{0,1:T(8,128)S(1)} %copy.44, ...), kind=kLoop, calls=%fused_computation.30 | loop fusion | flops 11534336 | bytes 12747264 | tf_op jit(solution)/shard_map/convert_element_type | solution.py:166
  489.2 4.1 copy.49
  (79 shorter events, 6.2 us)
Async XLA Ops:
  6.5 6.3 %copy-start = (bf16[64,4,128]{2,1,0:T(4,128)(2,1)S(1)}, bf16[64,4,128]{2,1,0:T(4,128)(2,1)}, u32[]{:S(2)}) copy-start(bf16[64,4,128]{2,1,0:T(4,128)(2,1)} %param.18) | copy-start | bytes 196612
  6.5 307.0 %all-gather.7.cloned.1.call-start = ((), (), s32[]{:S(2)}) async-start(), calls=%async_computation.1 | async-start | bytes 37748736 | tf_op jit(solution)/shard_map/all_gather | solution.py:12
  17.8 0.8 copy-start.5
  17.8 2.6 copy-start.10
  17.8 3.3 copy-start.3
  17.8 7.4 %copy-start.4 = (bf16[1,128,2,4,128]{4,3,2,1,0:T(4,128)(2,1)S(1)}, bf16[1,128,2,4,128]{4,3,2,1,0:T(4,128)(2,1)}, u32[]{:S(2)}) copy-start(bf16[1,128,2,4,128]{4,3,2,1,0:T(4,128)(2,1)} %param.21) | copy-start | bytes 786436
  17.8 359.8 %all-gather.5.cloned.1.call-start = ((), (), s32[]{:S(2)}) async-start(), calls=%async_computation | async-start | bytes 12582912 | tf_op jit(solution)/shard_map/all_gather | solution.py:12
  25.4 3.1 copy-start.8
  25.4 5.4 %copy-start.9 = (f32[1,1,128]{2,1,0:T(1,128)S(1)}, f32[1,1,128]{2,1,0:T(1,128)}, u32[]{:S(2)}) copy-start(f32[1,1,128]{2,1,0:T(1,128)} %get-tuple-element.329) | copy-start | bytes 1540
  28.3 439.5 %all-reduce.3.cloned.1.call-start = ((), (), s32[]{:S(2)}) async-start(), calls=%async_computation.2 | async-start | bytes 8519680 | tf_op jit(solution)/shard_map/psum | solution.py:29
  313.6 50.9 %copy-start.7 = (f32[128]{0:T(128)S(1)}, f32[128]{0:T(128)}, u32[]{:S(2)}) copy-start(f32[128]{0:T(128)} %fusion.43) | copy-start | bytes 1540
  467.8 4.7 copy-start.2
  472.4 8.2 %copy-start.6 = (f32[8192]{0:T(1024)S(1)}, f32[8192]{0:T(1024)}, u32[]{:S(2)}) copy-start(f32[8192]{0:T(1024)} %param.25) | copy-start | bytes 98308
  480.6 12.7 %copy-start.1 = (bf16[64,4,128]{2,1,0:T(4,128)(2,1)S(1)}, bf16[64,4,128]{2,1,0:T(4,128)(2,1)}, u32[]{:S(2)}) copy-start(bf16[64,4,128]{2,1,0:T(4,128)(2,1)} %param.18) | copy-start | bytes 196612
Sparse Core Ops, SparseCore 0:
  18.0 295.5 all-gather.6
  315.1 18.0 all-gather.4
  371.3 96.4 all-reduce.2
where the time goes:
time: 501 us; the launch traced here: 500 us
  waiting for transfers between devices  325 us (65%)
  other arithmetic  85.2 us (17%)
  blocking collectives  43 us (9%)
  matrix products  17.7 us (4%)
  between operations  14.7 us (3%)
  local copies, waits for them, and re-layouts  13.8 us (3%)
    all_gather x2, waiting for transfers between devices, carried_in(): everything = jax.tree.map(lambda part: lax.all_gather(part, axis), array)  246 us
    psum x1, waiting for transfers between devices, spread(): return lax.psum(jnp.where(mine, array, jnp.zeros_like(array)), axis)  79.2 us
    select_n x18, other arithmetic, turn(): return jax.tree.map(lambda a, b: jnp.where(reached, a, b), new, before)  61.4 us
    all_gather x3, blocking collectives, carried_in(): everything = jax.tree.map(lambda part: lax.all_gather(part, axis), array)  38.1 us
  transfers between devices with their start and end apart: 3, of which 2 were waited for; matrix products, arithmetic and copies ran while one was open for 17% of the time, Pallas kernels for 0%

commit v1 on v0

--- a/solution.py
+++ b/solution.py
@@ -5,28 +5,6 @@
 
 HEADS = 256
 HEAD_DIM = 64
-
-
-def carried_in(array, axis, combine, identity):
-    peers, mine = (lax.axis_size(axis), lax.axis_index(axis))
-    everything = jax.tree.map(lambda part: lax.all_gather(part, axis), array)
-    start = jax.tree.map(
-        lambda part, zero: jnp.broadcast_to(jnp.asarray(zero, part.dtype), part.shape),
-        array,
-        identity,
-    )
-
-    def turn(k, before):
-        reached = k < mine
-        new = combine(before, jax.tree.map(lambda part: part[k], everything))
-        return jax.tree.map(lambda a, b: jnp.where(reached, a, b), new, before)
-
-    return lax.fori_loop(0, peers, turn, start)
-
-
-def spread(array, axis, root):
-    mine = lax.axis_index(axis) == root
-    return lax.psum(jnp.where(mine, array, jnp.zeros_like(array)), axis)
 
 
 def block_state(rows_x, rows_b, rows_dt, decay_rate, groups):
@@ -78,19 +56,6 @@
     return outputs.reshape(length, head_count, head_size)
 
 
-def chain_link(earlier, later):
-    decay_all = jnp.exp(later[0])
-    return (
-        earlier[0] + later[0],
-        decay_all[:, None, None] * earlier[1] + later[1],
-        decay_all[:, None] * earlier[2] + later[2],
-    )
-
-
-def link_blocks(earlier, later):
-    return (earlier[0] + later[0], jnp.exp(later[0])[:, None, None] * earlier[1] + later[1])
-
-
 def local(
     prompt_x,
     prompt_b,
@@ -113,18 +78,13 @@
     prompt_total, prompt_state, prompt_carry, unused = block_state(
         prompt_x, prompt_b, prompt_dt, decay_rate, groups
     )
-    identity = (
-        jnp.zeros_like(prompt_total),
-        jnp.zeros_like(prompt_state),
-        jnp.zeros_like(prompt_carry),
-    )
-    before = carried_in(
-        (prompt_total, prompt_state, prompt_carry), ("req", "sp"), chain_link, identity
-    )
-    inclusive = chain_link(before, (prompt_total, prompt_state, prompt_carry))
-    prefix_state, prefix_carry = (
-        spread(inclusive[1], ("req", "sp"), lax.axis_size(("req", "sp")) - 1),
-        spread(inclusive[2], ("req", "sp"), lax.axis_size(("req", "sp")) - 1),
+    place = lax.axis_index(("req", "sp"))
+    totals = lax.all_gather(prompt_total, ("req", "sp"))
+    later = lax.broadcasted_iota(jnp.int32, totals.shape, 0) > place
+    remaining = jnp.exp(jnp.sum(jnp.where(later, totals, 0.0), axis=0))
+    prefix_state, prefix_carry = lax.psum(
+        (remaining[:, None, None] * prompt_state, remaining[:, None] * prompt_carry),
+        ("req", "sp"),
     )
     picked = lax.broadcasted_iota(jnp.int32, mult_table.shape, 0) == mult_idx[0]
     multiplier = jnp.sum(jnp.where(picked, mult_table, 0.0))
@@ -138,12 +98,7 @@
     block_total, local_state, carried, cumulative = block_state(
         steered, bmat, rows_dt, decay_rate, groups
     )
-    before_total, before_state = carried_in(
-        (block_total, local_state),
-        "sp",
-        link_blocks,
-        (jnp.zeros_like(block_total), jnp.zeros_like(local_state)),
-    )
+    before_total, before_state = lax.ppermute((block_total, local_state), "sp", [(0, 1)])
     inner = intra_block(steered, bmat, cmat, rows_dt, cumulative, groups)
     start_state = (
         prefix_state

time: 501 us -> 186 us (0.37)
  waiting for transfers between devices: 325 us -> 87.1 us
  other arithmetic: 85.2 us -> 25.8 us
  blocking collectives: 43 us -> 17.7 us
  starting transfers between devices: 0.09 us -> 6.66 us
    all_gather x2 -> x0, waiting for transfers between devices: 246 us -> none  [carried_in(): everything = jax.tree.map(lambda part: lax.all_gather(part, axis), array)]
    select_n x20 -> x0, other arithmetic: 68.1 us -> none  [the longest x18 61.4 us: turn(): return jax.tree.map(lambda a, b: jnp.where(reached, a, b), new, before)]
    all_gather x3 -> x1, blocking collectives: 38.1 us -> 12.7 us  [local(): totals = lax.all_gather(prompt_total, ('req', 'sp'))]
    psum x1, waiting for transfers between devices: 79.2 us -> 87.1 us  [local(): lax.psum((remaining[:, None, None] * prompt_state, remaining[:, None] * p...]
    ppermute x0 -> x2, starting transfers between devices: none -> 6.66 us  [local(): lax.ppermute((block_total, local_state), 'sp', [(0, 1)])]
  transfers between devices with their start and end apart: 3 -> 3, of which waited for: 2 -> 1; matrix products, arithmetic and copies ran while one was open for 17% -> 12% of each run, Pallas kernels for 0% -> 0%
where the time goes in v1:
time: 186 us; the launch traced here: 185 us
  waiting for transfers between devices  87.1 us (47%)
  other arithmetic  25.8 us (14%)
  blocking collectives  17.7 us (10%)
  local copies, waits for them, and re-layouts  16.7 us (9%)
  matrix products  16.4 us (9%)
  between operations  14.9 us (8%)
  starting transfers between devices  6.66 us (4%)
    psum x1, waiting for transfers between devices, local(): lax.psum((remaining[:, None, None] * prompt_state, remaining[:, None] * p...  87.1 us
    all_gather x1, blocking collectives, local(): totals = lax.all_gather(prompt_total, ('req', 'sp'))  12.7 us
    convert_element_type x1, other arithmetic, local(): (mixed * lax.rsqrt(meansq + 1e-05)[:, None] * norm_gain[None, :]).astype(...  8.54 us
    ppermute x2, starting transfers between devices, local(): lax.ppermute((block_total, local_state), 'sp', [(0, 1)])  6.66 us
    dot_general x1, matrix products, intra_block(): jnp.einsum('gqts,sgqp->tgqp', mixing, input_groups, preferred_element_typ...  6.31 us
    unnamed x29, local copies, waits for them, and re-layouts  6.24 us
    dot_general x2, matrix products, block_state(): jnp.einsum('tgqp,tgn->gqpn', scaled, rows_b, preferred_element_type=jnp.f...  5.64 us
    psum x1, blocking collectives, local(): total_squares = lax.psum(squares, 'tp')  4.92 us
  transfers between devices with their start and end apart: 3, of which 1 were waited for; matrix products, arithmetic and copies ran while one was open for 12% of the time, Pallas kernels for 0%

profile of v1, /device:TPU:0, one launch (start us, length us, event | category | flops | bytes accessed | tf_op | source)
XLA Modules:
  0.0 185.2 jit_solution(16064497047261371977)
XLA Ops:
  6.5 0.7 neg.9
  7.2 0.8 bitcast_multiply_fusion.4
  8.3 0.7 copy.42
  9.0 1.6 copy.43
  11.9 1.1 select_reduce_fusion
  13.1 1.3 fusion.34
  14.3 0.6 broadcast_multiply_fusion.1
  15.1 0.5 copy-done.5
  15.6 3.2 %copy.39 = bf16[1,128,8192]{1,2,0:T(8,128)(2,1)S(1)} copy(bf16[1,128,8192]{2,1,0:T(8,128)(2,1)} %param.16) | data formatting | bytes 4194304 | tf_op args[3]
  18.8 1.2 fusion.36
  20.0 1.6 fusion.37
  21.6 2.8 %fusion.17 = f32[4,32,64,128]{3,2,1,0:T(8,128)} fusion(f32[128,4,32]{0,2,1:T(8,128)S(1)} %get-tuple-element.14, bf16[1,128,1,4,128]{4,3,2,1,0:T(4,128)(2,1)S(1)} %get-tuple-element.8, f32[4,32,64]{2,1,0:T(8,128)S(1)} %mul.204, bf16[128,4,32,64]{0,3,2,1:T(8,128)(2,1)S(1)} %bitcast.77), kind=kOutput, calls=%fused_computation.27 | convolution fusion | flops 274726912 | bytes 6520832 | tf_op jit(solution)/shard_map/tgqp,tgn->gqpn/dot_general | solution.py:22
  24.3 4.3 %collective-permute-start.1 = (f32[128,64,128]{2,1,0:T(8,128)}, f32[128,64,128]{2,1,0:T(8,128)}, u32[]{:S(2)}, u32[]{:S(2)}) collective-permute-start(f32[128,64,128]{2,1,0:T(8,128)} %bitcast.24), channel_id=1, source_target_pairs={{0,1},{2,3},{4,5},{6,7},{8,9},{10,11},{12,13},{14,15},{16,17},{18,... | collective-permute-start | bytes 12582920 | tf_op jit(solution)/shard_map/ppermute | solution.py:101
  28.7 0.6 broadcast_multiply_fusion
  29.3 1.4 reduce_window_sum.26
  30.7 0.7 slice_bitcast_fusion.1
  31.4 1.4 exponential_multiply_fusion.1
  32.8 1.5 copy.45
  34.2 2.4 %copy.53 = f32[64,8192]{0,1:T(8,128)} copy(bf16[64,8192]{1,0:T(8,128)(2,1)S(1)} %copy-done.2) | data formatting | bytes 3145728 | tf_op jit(solution)/shard_map/reshape | solution.py:19
  36.6 12.7 %all-gather = f32[8,1,128]{2,1,0:T(1,128)S(1)} all-gather(f32[1,1,128]{2,1,0:T(1,128)S(1)} %get-tuple-element.17), channel_id=1, replica_groups=mesh['parts'=2,'req'=4,'tp'=2,'sp'=2] {'req','sp'}, dimensions={0}, use_global_device_ids=true | all-gather | bytes 4608 | tf_op jit(solution)/shard_map/all_gather | solution.py:82
  49.5 1.0 fusion.32
  50.5 0.7 bitcast_multiply_fusion.3
  51.2 2.9 %fusion.16 = f32[4,32,64,128]{3,2,1,0:T(8,128)S(1)} fusion(f32[64,4,32,64]{0,3,2,1:T(8,128)} %bitcast.80, f32[64,4,32]{0,2,1:T(8,128)} %bitcast.85, bf16[64,4,128,1]{2,1,0,3:T(4,128)(2,1)S(1)} %bitcast.76), kind=kOutput, calls=%fused_computation.26 | convolution fusion | flops 135266304 | bytes 6389760 | tf_op jit(solution)/shard_map/tgqp,tgn->gqpn/dot_general | solution.py:22
  54.1 2.3 %bitcast_multiply_fusion.1 = f32[128,64,128]{2,1,0:T(8,128)} fusion(f32[4,32,64,128]{3,2,1,0:T(8,128)S(1)} %fusion.16, f32[128]{0:T(128)S(1)} %exp.44), kind=kLoop, calls=%fused_computation.10 | loop fusion | flops 1048576 | bytes 8389120 | tf_op jit(solution)/shard_map/mul | solution.py:86
  56.4 2.3 %collective-permute-start = (f32[128]{0:T(128)S(1)}, f32[128]{0:T(128)S(1)}, u32[]{:S(2)}, u32[]{:S(2)}) collective-permute-start(f32[128]{0:T(128)S(1)} %get-tuple-element.15), channel_id=1, source_target_pairs={{0,1},{2,3},{4,5},{6,7},{8,9},{10,11},{12,13},{14,15},{16,17},{18,... | collective-permute-start | bytes 1544 | tf_op jit(solution)/shard_map/ppermute | solution.py:101
  59.0 6.3 %fusion.4 = f32[4,32,64,128]{3,2,1,0:T(8,128)} fusion(f32[4,32,128]{2,1,0:T(8,128)S(1)} %copy-done.10, f32[4,32,128]{2,1,0:T(8,128)S(1)} %copy-done.9, f32[4,128,128]{2,1,0:T(8,128)S(1)} %fusion.24, pred[128,128]{1,0:T(8,128)(4,1)S(1)} %iota_compare_fusion, f32[4,32,64]{2,1,0:T(8,128)S(1)} %mul.204, bf16[128,4,32,64]{0,3,2,1:T(8,128)(2,1)S(1)} %bitcast.78), kind=kOutput, calls=%fused_computation.7 | convolution fusion | flops 279969792 | bytes 6733824 | tf_op jit(solution)/shard_map/gqts,sgqp->tgqp/dot_general | solution.py:53
  65.8 87.1 %all-reduce.3.cloned.1.call-done = (f32[128,64,128]{2,1,0:T(8,128)}, f32[128,128]{1,0:T(8,128)}) async-done(((f32[128,64,128]{2,1,0:T(8,128)}, f32[128,128]{1,0:T(8,128)}), (f32[128,64,128]{2,1,0:T(8,128)}, f32[128,128]{1,0:T(8,128)})) %all-reduce.3.cloned.1.call-update) | async-done | bytes 4259856 | tf_op jit(solution)/shard_map/psum | solution.py:85
  152.9 4.4 %add_convert_fusion.1 = bf16[128,64,128]{2,1,0:T(8,128)(2,1)S(1)} fusion(f32[128,64,128]{2,1,0:T(8,128)} %collective-permute-done.1, f32[128,64,128]{2,1,0:T(8,128)} %get-tuple-element.5, f32[128,128]{1,0:T(8,128)} %get-tuple-element.6, f32[128,64]{1,0:T(8,128)S(1)} %mul.225, f32[128]{0:T(128)S(1)} %exp.43), kind=kLoop, calls=%fused_computation.18 | loop fusion | flops 5242880 | bytes 10584576 | tf_op jit(solution)/shard_map/convert_element_type | solution.py:108
  157.6 3.2 %fusion.3 = (f32[128]{0:T(128)S(1)}, f32[4,32,64,128]{3,2,1,0:T(8,128)}) fusion(f32[4,32,64,128]{3,2,1,0:T(8,128)S(1)} %copy-done.1, f32[4,32]{1,0:T(4,128)S(1)} %mul.242, f32[128,4,32]{0,2,1:T(8,128)S(1)} %copy-done.7, bf16[4,32,64,128]{3,2,1,0:T(8,128)(2,1)S(1)} %bitcast.83, bf16[1,128,1,4,128]{4,3,2,1,0:T(4,128)(2,1)S(1)} %get-tuple-element.7, ...), kind=kOutput, calls=%fused_computation.6 | convolution fusion | flops 278921088 | bytes 12813312 | tf_op jit(solution)/shard_map/tgn,gqpn->tgqp/dot_general | solution.py:109
  160.8 4.9 %psum.23 = f32[128]{0:T(128)S(1)} all-reduce(f32[128]{0:T(128)S(1)} %get-tuple-element.19), channel_id=1, replica_groups=mesh['parts'=2,'req'=4,'tp'=2,'sp'=2] {'tp'}, use_global_device_ids=true, to_apply=%region_8.9 | all-reduce | flops 128 | bytes 1024 | tf_op jit(solution)/shard_map/psum | solution.py:119
  165.7 8.5 %fusion.10 = bf16[1,128,8192]{1,2,0:T(8,128)(2,1)} fusion(f32[1,128,8192]{1,2,0:T(8,128)} %bitcast.81, f32[1,128,8192]{1,2,0:T(8,128)} %bitcast.82, f32[8192]{0:T(1024)S(1)} %copy-done.11, f32[128]{0:T(128)S(1)} %add_rsqrt_fusion, f32[8192]{0:T(1024)S(1)} %copy-done.6, f32[8192]{0:T(1024)S(1)} %mul.237, f32[128,128]{0,1:T(8,128)S(1)} %copy.44, ...), kind=kLoop, calls=%fused_computation.16 | loop fusion | flops 11534336 | bytes 12747264 | tf_op jit(solution)/shard_map/convert_element_type | solution.py:121
  174.3 4.1 %copy.49 = bf16[1,128,8192]{2,1,0:T(8,128)(2,1)} copy(bf16[1,128,8192]{1,2,0:T(8,128)(2,1)} %fusion.10) | data formatting | bytes 4194304 | tf_op jit(solution)/shard_map/convert_element_type | solution.py:121
  (47 shorter events, 1.4 us)
Async XLA Ops:
  6.5 42.9 %copy-start = (bf16[64,4,128]{2,1,0:T(4,128)(2,1)S(1)}, bf16[64,4,128]{2,1,0:T(4,128)(2,1)}, u32[]{:S(2)}) copy-start(bf16[64,4,128]{2,1,0:T(4,128)(2,1)} %param.14) | copy-start | bytes 196612
  6.5 146.3 %all-reduce.3.cloned.1.call-start = ((), (), s32[]{:S(2)}) async-start(), calls=%async_computation | async-start | bytes 8519680 | tf_op jit(solution)/shard_map/psum | solution.py:85
  8.2 6.7 %copy-start.3 = (f32[128,128]{1,0:T(8,128)}, f32[128,128]{1,0:T(8,128)S(1)}, u32[]{:S(2)}) copy-start(f32[128,128]{1,0:T(8,128)S(1)} %reduce_window_sum.24) | copy-start | bytes 196612
  15.0 0.6 copy-start.5
  18.8 9.8 %copy-start.8 = (f32[64,128]{1,0:T(8,128)S(1)}, f32[64,128]{1,0:T(8,128)}, u32[]{:S(2)}) copy-start(f32[64,128]{1,0:T(8,128)} %param.15) | copy-start | bytes 98308
  18.8 15.4 %copy-start.2 = (bf16[64,8192]{1,0:T(8,128)(2,1)S(1)}, bf16[64,8192]{1,0:T(8,128)(2,1)}, u32[]{:S(2)}) copy-start(bf16[64,8192]{1,0:T(8,128)(2,1)} %param.13) | copy-start | bytes 3145732
  24.3 128.5 %collective-permute-start.1 = (f32[128,64,128]{2,1,0:T(8,128)}, f32[128,64,128]{2,1,0:T(8,128)}, u32[]{:S(2)}, u32[]{:S(2)}) collective-permute-start(f32[128,64,128]{2,1,0:T(8,128)} %bitcast.24), channel_id=1, source_target_pairs={{0,1},{2,3},{4,5},{6,7},{8,9},{10,11},{12,13},{14,15},{16,17},{18,... | collective-permute-start | bytes 12582920 | tf_op jit(solution)/shard_map/ppermute | solution.py:101
  56.3 2.6 %copy-start.9 = (f32[4,32,128]{2,1,0:T(8,128)S(1)}, f32[4,32,128]{2,1,0:T(8,128)}, u32[]{:S(2)}) copy-start(f32[4,32,128]{2,1,0:T(8,128)} %get-tuple-element.12) | copy-start | bytes 196612
  56.3 2.6 %copy-start.10 = (f32[4,32,128]{2,1,0:T(8,128)S(1)}, f32[4,32,128]{2,1,0:T(8,128)}, u32[]{:S(2)}) copy-start(f32[4,32,128]{2,1,0:T(8,128)} %get-tuple-element.13) | copy-start | bytes 196612
  56.4 9.4 %collective-permute-start = (f32[128]{0:T(128)S(1)}, f32[128]{0:T(128)S(1)}, u32[]{:S(2)}, u32[]{:S(2)}) collective-permute-start(f32[128]{0:T(128)S(1)} %get-tuple-element.15), channel_id=1, source_target_pairs={{0,1},{2,3},{4,5},{6,7},{8,9},{10,11},{12,13},{14,15},{16,17},{18,... | collective-permute-start | bytes 1544 | tf_op jit(solution)/shard_map/ppermute | solution.py:101
  59.0 6.3 %copy-start.6 = (f32[8192]{0:T(1024)S(1)}, f32[8192]{0:T(1024)}, u32[]{:S(2)}) copy-start(f32[8192]{0:T(1024)} %copy-done.5) | copy-start | bytes 98308
  59.0 6.4 %copy-start.4 = (f32[128,128]{1,0:T(8,128)S(1)}, f32[128,128]{1,0:T(8,128)}, u32[]{:S(2)}) copy-start(f32[128,128]{1,0:T(8,128)} %copy-done.3) | copy-start | bytes 196612
  59.0 6.4 %copy-start.12 = (f32[128]{0:T(128)S(1)}, f32[128]{0:T(128)}, u32[]{:S(2)}) copy-start(f32[128]{0:T(128)} %param.20) | copy-start | bytes 1540
  152.9 4.7 %copy-start.1 = (f32[4,32,64,128]{3,2,1,0:T(8,128)S(1)}, f32[4,32,64,128]{3,2,1,0:T(8,128)}, u32[]{:S(2)}) copy-start(f32[4,32,64,128]{3,2,1,0:T(8,128)} %fusion.4) | copy-start | bytes 12582916
  152.9 4.7 %copy-start.7 = (f32[128,4,32]{0,2,1:T(8,128)S(1)}, f32[128,4,32]{0,2,1:T(8,128)}, u32[]{:S(2)}) copy-start(f32[128,4,32]{0,2,1:T(8,128)} %get-tuple-element.11) | copy-start | bytes 196612
  157.6 8.2 %copy-start.11 = (f32[8192]{0:T(1024)S(1)}, f32[8192]{0:T(1024)}, u32[]{:S(2)}) copy-start(f32[8192]{0:T(1024)} %param.21) | copy-start | bytes 98308
Sparse Core Ops, SparseCore 0:
  56.5 96.3 all-reduce.2

commit v2 on v1

v2 whole, which is shorter than its diff:
```python
import functools

import jax
import jax.numpy as jnp
from jax import lax
from jax.experimental import pallas as pl
from jax.experimental.pallas import tpu as pltpu
from jax.sharding import PartitionSpec as P

MESH = pl.DeviceIdType.MESH
F32 = jnp.float32
BF16 = jnp.bfloat16
HIGHEST = lax.Precision.HIGHEST
WIDTH = 256


def dot(a, b):
    return jnp.dot(a, b, preferred_element_type=F32)


def halves(value):
    lead = value.astype(BF16)
    rest = (value - lead.astype(F32)).astype(BF16)
    return jnp.concatenate([lead, rest], axis=1)


def running_sum(rows):
    length = rows.shape[0]
    lower = lax.broadcasted_iota(jnp.int32, (length, length), 0) >= lax.broadcasted_iota(
        jnp.int32, (length, length), 1
    )
    return jnp.dot(
        jnp.where(lower, 1.0, 0.0).astype(F32),
        rows,
        precision=HIGHEST,
        preferred_element_type=F32,
    )


def kernel(
    R,
    TP,
    NCK,
    px,
    pbt,
    pdt,
    cx,
    cbt,
    cc,
    cdt,
    rate,
    skip,
    mv,
    out,
    ss,
    whl,
    colhl,
    rowhl,
    row2hl,
    skiphl,
    cterm,
    gmat,
    row2x,
    tots,
    ctot,
    ctot_in,
    st0s,
    st0r,
    s_sib,
    s_rec,
    s_own,
    s_lin,
    s_lout,
    s_rin,
    s_rout,
    s_tot,
    s_ag,
    c_all,
    c_rec,
    c_own,
    c_lin,
    c_lout,
    c_rin,
    c_rout,
    c_tot,
    c_ag,
    incb,
    ssacc,
    ssl,
    t_send,
    t_recv,
    x_send,
    x_recv,
    l_send,
    l_recv,
    r_send,
    r_recv,
    a_send,
    a_recv,
    z_send,
    z_recv,
    d_send,
    d_recv,
    p_send,
    p_recv,
):
    i = lax.axis_index("req")
    s = lax.axis_index("sp")
    x = lax.axis_index("tp")
    me = i * 2 + s
    hr = R - 1 - i
    far = jnp.maximum(i, hr)
    H = pdt.shape[1]
    C = px.shape[1]
    Gd = pbt.shape[0]
    N = pbt.shape[1]
    T = cx.shape[0]
    half = C // 2
    head = C // H
    gw = C // Gd
    per_group = H // Gd
    nh = N // 2
    sib = {"sp": 1 - s}

    def each(count, skip_index, body):
        def turn(j, carry):
            @pl.when(j != skip_index)
            def _():
                body(j)

            return carry

        lax.fori_loop(0, count, turn, 0)

    def peer(j):
        return {"req": j // 2, "sp": j % 2}

    def remote(src, dst, send, recv, device):
        return pltpu.make_async_remote_copy(
            src_ref=src,
            dst_ref=dst,
            send_sem=send,
            recv_sem=recv,
            device_id=device,
            device_id_type=MESH,
        )

    barrier = pltpu.get_barrier_semaphore()
    each(
        2 * R,
        me,
        lambda j: pl.semaphore_signal(barrier, inc=1, device_id=peer(j), device_id_type=MESH),
    )
    each(
        TP,
        x,
        lambda j: pl.semaphore_signal(barrier, inc=1, device_id={"tp": j}, device_id_type=MESH),
    )
    cum = running_sum(-rate[...] * pdt[...])
    total = cum[pdt.shape[0] - 1 :, :]
    tots[me] = jnp.broadcast_to(total, (8, H))
    pl.semaphore_wait(barrier, 2 * R - 1 + TP - 1)

    def tot_copy(j, slot):
        return remote(tots.at[slot], tots.at[slot], t_send.at[j], t_recv.at[slot], peer(j))

    each(2 * R, me, lambda j: tot_copy(j, me).start())

    ccum = running_sum(-rate[...] * cdt[...])
    ctot[...] = jnp.broadcast_to(ccum[T - 1 :, :], (8, H))

    def d_copy():
        return remote(ctot, ctot_in, d_send.at[0], d_recv.at[0], sib)

    @pl.when(s == 0)
    def _():
        d_copy().start()

    colhl[...] = halves(jnp.exp(-ccum) * cdt[...])
    rowhl[...] = halves(jnp.exp(ccum))
    skiphl[...] = halves(jnp.broadcast_to(skip[...], (8, H)))
    ssacc[...] = jnp.zeros_like(ssacc)

    each(2 * R, me, lambda j: tot_copy(j, j).wait_recv())
    every = tots[...]
    after = lax.broadcasted_iota(jnp.int32, every.shape, 0) > me
    suffix = jnp.sum(jnp.where(after, every, 0.0), axis=0)[0:1, :]
    weight = jnp.exp(suffix + total - cum) * pdt[...]
    whl[...] = halves(weight)

    carry = jnp.zeros((N, H), F32)
    lane_group = lax.broadcasted_iota(jnp.int32, (N, H), 1)
    for g in range(Gd):
        inside = (lane_group >= g * per_group) & (lane_group < (g + 1) * per_group)
        part = jnp.dot(
            pbt[g].astype(F32), weight, precision=HIGHEST, preferred_element_type=F32
        )
        carry = jnp.where(inside, part, carry)
    c_all[0] = carry[:nh]
    c_all[1] = carry[nh:]

    def x_copy(src, dst, k):
        return remote(src, dst, x_send.at[k], x_recv.at[k], sib)

    def carry_x():
        return x_copy(c_all.at[1 - s], c_rec, NCK)

    def state_x(k):
        return x_copy(s_sib.at[k], s_rec.at[k], k)

    def l_copy(src, dst, k):
        return remote(src, dst, l_send.at[k], l_recv.at[k], {"req": jnp.minimum(i + 1, R - 1)})

    def r_copy(src, dst, k):
        return remote(src, dst, r_send.at[k], r_recv.at[k], {"req": jnp.maximum(i - 1, 0)})

    def carry_l():
        return l_copy(c_lout, c_lin, NCK)

    def state_l(k):
        return l_copy(s_lout.at[k], s_lin.at[k], k)

    def carry_r():
        return r_copy(c_rout, c_rin, NCK)

    def state_r(k):
        return r_copy(s_rout.at[k], s_rin.at[k], k)

    def carry_a():
        return remote(c_tot, c_ag, a_send.at[NCK], a_recv.at[NCK], sib)

    def state_a(k):
        return remote(s_tot.at[k], s_ag.at[k], a_send.at[k], a_recv.at[k], sib)

    def z_copy(j):
        return remote(st0s.at[j], st0r.at[j], z_send.at[j], z_recv.at[j], sib)

    carry_x().start()

    def chosen(first_head):
        row = lax.broadcasted_iota(jnp.int32, (2 * H, WIDTH), 0)
        row = jnp.where(row >= H, row - H, row)
        shift = head.bit_length() - 1
        col = lax.shift_right_logical(
            lax.broadcasted_iota(jnp.int32, (2 * H, WIDTH), 1), shift
        )
        return jnp.where(row == col + first_head, 1.0, 0.0).astype(BF16)

    def place(owner, k):
        return pl.multiple_of(owner * half + k * WIDTH, WIDTH)

    def slice_at(base):
        return pl.ds(base, WIDTH)

    def prompt_chunk(owner, k):
        base = place(owner, k)
        spread = dot(whl[...], chosen(base // head))
        scaled = (px[:, slice_at(base)].astype(F32) * spread).astype(BF16)
        return dot(pbt[base // gw], scaled)

    def cont_chunk(owner, k):
        base = place(owner, k)
        j = owner * NCK + k
        g = base // gw
        pick = chosen(base // head)
        steered = (cx[:, slice_at(base)].astype(F32) + mv[:, slice_at(base)]).astype(BF16)
        wide = steered.astype(F32)
        scaled = (wide * dot(colhl[...], pick)).astype(BF16)
        inner = dot(gmat[g], scaled)
        gain = dot(skiphl[...], pick)[0:1, :]
        out[:, slice_at(base)] = dot(rowhl[...], pick) * inner + gain * wide
        row2x[j] = dot(row2hl[...], pick)

        @pl.when(s == 0)
        def _():
            st0s[j] = dot(cbt[g], scaled)
            z_copy(j).start()

    def finish(owner, k, ready):
        base = place(owner, k)
        j = owner * NCK + k
        g = base // gw

        @pl.when(s == 0)
        def _():
            incb[...] = ready[k].astype(BF16)

        @pl.when(s == 1)
        def _():
            z_copy(j).wait_recv()
            incb[...] = (ready[k] + st0r[j]).astype(BF16)

        steer = dot(cterm[...], chosen(base // head)) * mv[:, slice_at(base)]
        y = dot(cc[g], incb[...]) + steer
        mixed = out[:, slice_at(base)] + row2x[j] * y
        out[:, slice_at(base)] = mixed
        square = mixed * mixed
        folded = square[:, :128]
        for q in range(1, WIDTH // 128):
            folded = folded + square[:, q * 128 : (q + 1) * 128]
        ssacc[...] += folded

    lower = lax.broadcasted_iota(jnp.int32, (T, T), 0) >= lax.broadcasted_iota(
        jnp.int32, (T, T), 1
    )
    for g in range(Gd):
        gmat[g] = jnp.where(lower, dot(cc[g], cbt[g]), 0.0).astype(BF16)

    @pl.when(s == 0)
    def _():
        row2hl[...] = rowhl[...]

    @pl.when(s == 1)
    def _():
        d_copy().wait_recv()
        row2hl[...] = halves(jnp.exp(ccum + ctot_in[0:1, :]))

    def push_left_sum(own, lin, lout, copy):
        @pl.when(i > 0)
        def _():
            copy().wait_recv()

        @pl.when(i == 0)
        def _():
            lout[...] = own[...]
            copy().start()

        @pl.when((i > 0) & (i < R - 1))
        def _():
            lout[...] = own[...] + lin[...]
            copy().start()

    def push_right_sum(own, rin, rout, copy):
        @pl.when(i < R - 1)
        def _():
            copy().wait_recv()

        @pl.when(i == R - 1)
        def _():
            rout[...] = own[...]
            copy().start()

        @pl.when((i > 0) & (i < R - 1))
        def _():
            rout[...] = own[...] + rin[...]
            copy().start()

    def close(own, lin, rin, tot, copy):
        @pl.when(i == 0)
        def _():
            tot[...] = own[...] + rin[...]

        @pl.when(i == R - 1)
        def _():
            tot[...] = own[...] + lin[...]

        @pl.when((i > 0) & (i < R - 1))
        def _():
            tot[...] = own[...] + lin[...] + rin[...]

        copy().start()

    def within(k):
        return (k >= 0) & (k < NCK)

    def step(m, unused):
        @pl.when(m < NCK)
        def _():
            s_sib[m] = prompt_chunk(1 - s, m)
            state_x(m).start()
            s_own[m] = prompt_chunk(s, m)

        @pl.when(m == 0)
        def _():
            carry_x().wait_recv()
            c_own[...] = c_all[s] + c_rec[...]

        @pl.when(within(m - 1))
        def _():
            state_x(m - 1).wait_recv()
            s_own[m - 1] = s_own[m - 1] + s_rec[m - 1]

        @pl.when(m == i)
        def _():
            push_left_sum(c_own, c_lin, c_lout, carry_l)

        @pl.when(m == hr)
        def _():
            push_right_sum(c_own, c_rin, c_rout, carry_r)

        kl = m - 1 - i

        @pl.when(within(kl))
        def _():
            push_left_sum(
                s_own.at[kl], s_lin.at[kl], s_lout.at[kl], functools.partial(state_l, kl)
            )

        kr = m - 1 - hr

        @pl.when(within(kr))
        def _():
            push_right_sum(
                s_own.at[kr], s_rin.at[kr], s_rout.at[kr], functools.partial(state_r, kr)
            )

        @pl.when(m < NCK)
        def _():
            cont_chunk(s, m)
            cont_chunk(1 - s, m)

        @pl.when(m == far)
        def _():
            close(c_own, c_lin, c_rin, c_tot, carry_a)

        @pl.when(m == far + 1)
        def _():
            carry_a().wait_recv()
            low = jnp.where(s == 0, c_tot[...], c_ag[...])
            high = jnp.where(s == 0, c_ag[...], c_tot[...])
            both = jnp.concatenate([low, high], axis=0)
            lane = lax.broadcasted_iota(jnp.int32, (T, H), 1)
            seen = jnp.zeros((T, H), F32)
            for g in range(Gd):
                inside = (lane >= g * per_group) & (lane < (g + 1) * per_group)
                part = jnp.dot(
                    cc[g].astype(F32), both, precision=HIGHEST, preferred_element_type=F32
                )
                seen = jnp.where(inside, part, seen)
            cterm[...] = halves(seen)

        kt = m - 1 - far

        @pl.when(within(kt))
        def _():
            close(
                s_own.at[kt],
                s_lin.at[kt],
                s_rin.at[kt],
                s_tot.at[kt],
                functools.partial(state_a, kt),
            )
            finish(s, kt, s_tot)

        kf = kt - 1

        @pl.when(within(kf))
        def _():
            state_a(kf).wait_recv()
            finish(1 - s, kf, s_ag)

        return unused

    lax.fori_loop(0, NCK + R + 1, step, 0)

    ssl[x] = lax.dot_general(
        jnp.ones((8, 128), F32),
        ssacc[...],
        (((1,), (1,)), ((), ())),
        precision=HIGHEST,
        preferred_element_type=F32,
    )

    def p_copy(j, slot):
        return remote(ssl.at[slot], ssl.at[slot], p_send.at[j], p_recv.at[slot], {"tp": j})

    each(TP, x, lambda j: p_copy(j, x).start())

    def sent(k, unused):
        state_x(k).wait_send()
        state_a(k).wait_send()

        @pl.when(i < R - 1)
        def _():
            state_l(k).wait_send()

        @pl.when(i > 0)
        def _():
            state_r(k).wait_send()

        @pl.when(s == 0)
        def _():
            z_copy(k).wait_send()
            z_copy(k + NCK).wait_send()

        return unused

    lax.fori_loop(0, NCK, sent, 0)
    carry_x().wait_send()
    carry_a().wait_send()

    @pl.when(i < R - 1)
    def _():
        carry_l().wait_send()

    @pl.when(i > 0)
    def _():
        carry_r().wait_send()

    @pl.when(s == 0)
    def _():
        d_copy().wait_send()

    each(2 * R, me, lambda j: tot_copy(j, me).wait_send())
    each(TP, x, lambda j: p_copy(j, j).wait_recv())
    ss[...] = jnp.sum(ssl[...], axis=0)
    each(TP, x, lambda j: p_copy(j, x).wait_send())


def local(
    prompt_x,
    prompt_b,
    prompt_dt,
    cont_x,
    cont_bc,
    cont_dt,
    decay_rate,
    skip_gain,
    norm_gain,
    steer_vecs,
    mult_table,
    mult_idx,
    behav_idx,
):
    R, TP = lax.axis_size("req"), lax.axis_size("tp")
    H = decay_rate.shape[0]
    tokens, C = prompt_x.shape
    Gd, N = prompt_b.shape[1:]
    T = cont_x.shape[1]
    NCK = C // 2 // WIDTH
    picked = lax.broadcasted_iota(jnp.int32, mult_table.shape, 0) == mult_idx[0]
    multiplier = jnp.sum(jnp.where(picked, mult_table, 0.0))
    choose = lax.broadcasted_iota(jnp.int32, (steer_vecs.shape[0], 1), 0) == behav_idx[0]
    vector = jnp.sum(jnp.where(choose, steer_vecs, 0.0), axis=0)
    args = (
        prompt_x,
        jnp.transpose(prompt_b, (1, 2, 0)),
        prompt_dt,
        cont_x[0],
        jnp.transpose(cont_bc[0, :, 0], (1, 2, 0)),
        jnp.transpose(cont_bc[0, :, 1], (1, 0, 2)),
        cont_dt[0],
        decay_rate[None],
        skip_gain[None],
        (multiplier * vector)[None],
    )
    vmem, dma = pltpu.VMEM, pltpu.SemaphoreType.DMA
    part = (NCK, N, WIDTH)
    carried = (N // 2, H)
    scratch = (
        [vmem((tokens, 2 * H), BF16)]
        + [vmem((T, 2 * H), BF16)] * 3
        + [vmem((8, 2 * H), BF16), vmem((T, 2 * H), BF16), vmem((Gd, T, T), BF16)]
        + [vmem((2 * NCK, T, WIDTH), F32)]
        + [vmem((2 * R, 8, H), F32)]
        + [vmem((8, H), F32)] * 2
        + [vmem((2 * NCK, N, WIDTH), F32)] * 2
        + [vmem(part, F32)] * 9
        + [vmem((2,) + carried, F32)]
        + [vmem(carried, F32)] * 8
        + [vmem((N, WIDTH), BF16), vmem((T, 128), F32), vmem((TP, 8, T), F32)]
        + [dma((2 * R,))] * 2
        + [dma((NCK + 1,))] * 8
        + [dma((2 * NCK,))] * 2
        + [dma((1,))] * 2
        + [dma((TP,))] * 2
    )
    mixed, squares = pl.pallas_call(
        functools.partial(kernel, R, TP, NCK),
        out_shape=(
            jax.ShapeDtypeStruct((T, C), F32),
            jax.ShapeDtypeStruct((8, T), F32),
        ),
        in_specs=[pl.BlockSpec(memory_space=pltpu.VMEM)] * len(args),
        out_specs=(pl.BlockSpec(memory_space=pltpu.VMEM),) * 2,
        scratch_shapes=scratch,
        compiler_params=pltpu.CompilerParams(
            collective_id=0, has_side_effects=True, vmem_limit_bytes=60 * 1024 * 1024
        ),
        name="sweep",
    )(*args)
    meansq = squares[0] / (norm_gain.shape[0] * TP)
    return (mixed * lax.rsqrt(meansq + 1e-05)[:, None] * norm_gain[None, :]).astype(BF16)[None]


def solution(mesh):
    return jax.shard_map(
        local,
        mesh=mesh,
        in_specs=(
            P(("parts", "req", "sp"), "tp"),
            P(("parts", "req", "sp"), "tp", None),
            P(("parts", "req", "sp"), "tp"),
            P(("parts", "req"), "sp", "tp"),
            P(("parts", "req"), "sp", None, "tp", None),
            P(("parts", "req"), "sp", "tp"),
            P("tp"),
            P("tp"),
            P("tp"),
            P(None, "tp"),
            P(),
            P(("parts", "req")),
            P(("parts", "req")),
        ),
        out_specs=P(("parts", "req"), "sp", "tp"),
        check_vma=False,
    )
```

time: 186 us -> 113 us (0.61)
  Pallas kernels: 0 us -> 99.1 us
  waiting for transfers between devices: 87.1 us -> 0 us
  blocking collectives: 17.7 us -> 0 us
  other arithmetic: 25.8 us -> 8.31 us
  matrix products: 16.4 us -> 0 us
  between operations: 14.9 us -> 1.33 us
  local copies, waits for them, and re-layouts: 16.7 us -> 4.09 us
  starting transfers between devices: 6.66 us -> 0 us
    pallas_call x0 -> x1, Pallas kernels: none -> 99.1 us  [local(): pl.pallas_call(functools.partial(kernel, R, TP, NCK), out_shape=(jax.Shap...]
    psum x1 -> x0, waiting for transfers between devices: 87.1 us -> none  [local(): lax.psum((remaining[:, None, None] * prompt_state, remaining[:, None] * p...]
    dot_general x6 -> x0, matrix products: 16.4 us -> none  [the longest x1 6.31 us: intra_block(): jnp.einsum('gqts,sgqp->tgqp', mixing, input_groups, preferred_element_typ...]
    convert_element_type x2 -> x0, other arithmetic: 13 us -> none  [the longest x1 8.54 us: local(): (mixed * lax.rsqrt(meansq + 1e-05)[:, None] * norm_gain[None, :]).astype(...]
    all_gather x1 -> x0, blocking collectives: 12.7 us -> none  [local(): totals = lax.all_gather(prompt_total, ('req', 'sp'))]
    ppermute x2 -> x0, starting transfers between devices: 6.66 us -> none  [local(): lax.ppermute((block_total, local_state), 'sp', [(0, 1)])]
    mul x6 -> x1, other arithmetic: 6.43 us -> 1.25 us  [local(): multiplier * vector]
    psum x1 -> x0, blocking collectives: 4.92 us -> none  [local(): total_squares = lax.psum(squares, 'tp')]
  transfers between devices with their start and end apart: 3 -> 0, of which waited for: 1 -> 0; matrix products, arithmetic and copies ran while one was open for 12% -> 0% of each run, Pallas kernels for 0% -> 0%
where the time goes in v2:
time: 113 us
  Pallas kernels  99.1 us (88%)
  other arithmetic  8.31 us (7%)
  local copies, waits for them, and re-layouts  4.09 us (4%)
  between operations  1.33 us (1%)
    pallas_call x1, Pallas kernels, local(): pl.pallas_call(functools.partial(kernel, R, TP, NCK), out_shape=(jax.Shap...  99.1 us
    broadcast_in_dim x1, other arithmetic, local(): (mixed * lax.rsqrt(meansq + 1e-05)[:, None] * norm_gain[None, :]).astype(...  4.01 us
    unnamed x5, local copies, waits for them, and re-layouts  3.03 us

profile of v2, /device:TPU:0, one launch (start us, length us, event | category | flops | bytes accessed | tf_op | source)
XLA Modules:
  0.0 112.8 jit_solution(9381836973816488970)
XLA Ops:
  0.0 0.0 copy-start
  1.3 1.3 %fusion.1 = f32[]{:T(128)} fusion(f32[9]{0:T(128)} %param.23, s32[]{:T(128)} %bitcast.20), kind=kLoop, calls=%fused_computation.6 | loop fusion | flops 26 | bytes 44 | tf_op jit(solution)/shard_map/reduce_sum | solution.py:532
  2.6 1.1 select_reduce_fusion
  3.7 1.2 %broadcast_multiply_fusion = f32[8192]{0:T(1024)} fusion(f32[8192]{0:T(1024)S(1)} %select_reduce_fusion, f32[]{:T(128)} %fusion.1), kind=kLoop, calls=%fused_computation.4 | loop fusion | flops 8192 | bytes 65540 | tf_op jit(solution)/shard_map/mul | solution.py:545
  4.9 1.6 %copy.14 = bf16[64,4,128]{0,2,1:T(8,128)(2,1)} copy(bf16[64,4,128]{2,1,0:T(4,128)(2,1)} %param.14) | data formatting | bytes 131072 | tf_op args[1]
  6.5 1.1 fusion.2
  7.6 0.7 copy.20
  8.3 0.8 copy.17
  9.0 99.1 %sweep.1 = (f32[128,8192]{1,0:T(8,128)}, f32[8,128]{1,0:T(8,128)}) custom-call(bf16[64,8192]{1,0:T(8,128)(2,1)} %px.1, bf16[4,128,64]{2,1,0:T(8,128)(2,1)} %bitcast.23, f32[64,128]{1,0:T(8,128)} %pdt.1, bf16[128,8192]{1,0:T(8,128)(2,1)} %bitcast.22, bf16[4,128,128]{2,1,0:T(8,128)(2,1)} %bitcast.25, bf16[4,128,128]{2,1,0:T(8,128)(2,1)} %bitcast.24, ...), custom_call_target="tpu_custom_call" | custom-call | tf_op jit(solution)/shard_map/sweep/pallas_call | solution.py:568
  108.1 0.7 rsqrt_bitcast_fusion
  108.8 0.0 copy-done
  108.8 4.0 %fusion = bf16[1,128,8192]{2,1,0:T(8,128)(2,1)} fusion(f32[128,8192]{1,0:T(8,128)} %get-tuple-element.7, f32[8192]{0:T(1024)S(1)} %copy-done, f32[128]{0:T(128)S(1)} %rsqrt_bitcast_fusion), kind=kLoop, calls=%fused_computation.1 | loop fusion | flops 3145728 | bytes 6324736 | tf_op jit(solution)/shard_map/broadcast_in_dim | solution.py:583
  (1 shorter events, 0.0 us)
Async XLA Ops:
  0.0 108.8 %copy-start = (f32[8192]{0:T(1024)S(1)}, f32[8192]{0:T(1024)}, u32[]{:S(2)}) copy-start(f32[8192]{0:T(1024)} %param.21) | copy-start | bytes 98308

commit v3 on v2

--- a/solution.py
+++ b/solution.py
@@ -12,6 +12,9 @@
 BF16 = jnp.bfloat16
 HIGHEST = lax.Precision.HIGHEST
 WIDTH = 256
+AHEAD = 2
+SKEW = 2
+LAG = 2
 
 
 def dot(a, b):
@@ -42,15 +45,17 @@
     TP,
     NCK,
     px,
-    pbt,
+    pb,
     pdt,
     cx,
-    cbt,
-    cc,
+    cbc,
     cdt,
     rate,
     skip,
-    mv,
+    vecs,
+    table,
+    mult_at,
+    behav_at,
     out,
     ss,
     whl,
@@ -87,6 +92,10 @@
     incb,
     ssacc,
     ssl,
+    mv,
+    pbt,
+    cbt,
+    cc,
     t_send,
     t_recv,
     x_send,
@@ -112,8 +121,7 @@
     far = jnp.maximum(i, hr)
     H = pdt.shape[1]
     C = px.shape[1]
-    Gd = pbt.shape[0]
-    N = pbt.shape[1]
+    Gd, N = pb.shape[1:]
     T = cx.shape[0]
     half = C // 2
     head = C // H
@@ -180,6 +188,20 @@
     rowhl[...] = halves(jnp.exp(ccum))
     skiphl[...] = halves(jnp.broadcast_to(skip[...], (8, H)))
     ssacc[...] = jnp.zeros_like(ssacc)
+    entry = lax.broadcasted_iota(jnp.int32, table.shape, 1) == mult_at[0]
+    multiplier = jnp.sum(jnp.where(entry, table[...], 0.0), axis=1, keepdims=True)
+    wanted = lax.broadcasted_iota(jnp.int32, vecs.shape, 0) == behav_at[0]
+    mv[...] = multiplier * jnp.sum(jnp.where(wanted, vecs[...], 0.0), axis=0, keepdims=True)
+    for g in range(Gd):
+        pbt[g] = pb[:, g, :].astype(F32).T.astype(BF16)
+        cbt[g] = cbc[:, 0, g, :].astype(F32).T.astype(BF16)
+        cc[g] = cbc[:, 1, g, :]
+
+    lower = lax.broadcasted_iota(jnp.int32, (T, T), 0) >= lax.broadcasted_iota(
+        jnp.int32, (T, T), 1
+    )
+    for g in range(Gd):
+        gmat[g] = jnp.where(lower, dot(cc[g], cbt[g]), 0.0).astype(BF16)
 
     each(2 * R, me, lambda j: tot_copy(j, j).wait_recv())
     every = tots[...]
@@ -215,16 +237,18 @@
         return remote(src, dst, r_send.at[k], r_recv.at[k], {"req": jnp.maximum(i - 1, 0)})
 
     def carry_l():
-        return l_copy(c_lout, c_lin, NCK)
-
-    def state_l(k):
-        return l_copy(s_lout.at[k], s_lin.at[k], k)
+        return l_copy(c_lout, c_lin, 2 * NCK)
+
+    def state_l(k, q):
+        rows = pl.ds(q * nh, nh)
+        return l_copy(s_lout.at[k, rows], s_lin.at[k, rows], k + q * NCK)
 
     def carry_r():
-        return r_copy(c_rout, c_rin, NCK)
-
-    def state_r(k):
-        return r_copy(s_rout.at[k], s_rin.at[k], k)
+        return r_copy(c_rout, c_rin, 2 * NCK)
+
+    def state_r(k, q):
+        rows = pl.ds(q * nh, nh)
+        return r_copy(s_rout.at[k, rows], s_rin.at[k, rows], k + q * NCK)
 
     def carry_a():
         return remote(c_tot, c_ag, a_send.at[NCK], a_recv.at[NCK], sib)
@@ -300,21 +324,6 @@
             folded = folded + square[:, q * 128 : (q + 1) * 128]
         ssacc[...] += folded
 
-    lower = lax.broadcasted_iota(jnp.int32, (T, T), 0) >= lax.broadcasted_iota(
-        jnp.int32, (T, T), 1
-    )
-    for g in range(Gd):
-        gmat[g] = jnp.where(lower, dot(cc[g], cbt[g]), 0.0).astype(BF16)
-
-    @pl.when(s == 0)
-    def _():
-        row2hl[...] = rowhl[...]
-
-    @pl.when(s == 1)
-    def _():
-        d_copy().wait_recv()
-        row2hl[...] = halves(jnp.exp(ccum + ctot_in[0:1, :]))
-
     def push_left_sum(own, lin, lout, copy):
         @pl.when(i > 0)
         def _():
@@ -364,56 +373,77 @@
         return (k >= 0) & (k < NCK)
 
     def step(m, unused):
+        kb = m - AHEAD
+
+        @pl.when(kb == -1)
+        def _():
+            carry_x().wait_recv()
+            c_own[...] = c_all[s] + c_rec[...]
+
+            @pl.when(s == 0)
+            def _():
+                row2hl[...] = rowhl[...]
+
+            @pl.when(s == 1)
+            def _():
+                d_copy().wait_recv()
+                row2hl[...] = halves(jnp.exp(ccum + ctot_in[0:1, :]))
+
+        @pl.when(within(kb))
+        def _():
+            state_x(kb).wait_recv()
+            s_own[kb] = s_own[kb] + s_rec[kb]
+
+        kl = kb - SKEW * i
+        kr = kb - SKEW * hr
+        kt = kb - SKEW * far
+        kf = kt - LAG
+
+        @pl.when(kl == -1)
+        def _():
+            push_left_sum(c_own, c_lin, c_lout, carry_l)
+
+        @pl.when(kr == -1)
+        def _():
+            push_right_sum(c_own, c_rin, c_rout, carry_r)
+
+        for q in range(2):
+            rows = pl.ds(q * nh, nh)
+
+            @pl.when(within(kl))
+            def _():
+                push_left_sum(
+                    s_own.at[kl, rows],
+                    s_lin.at[kl, rows],
+                    s_lout.at[kl, rows],
+                    functools.partial(state_l, kl, q),
+                )
+
+            @pl.when(within(kr))
+            def _():
+                push_right_sum(
+                    s_own.at[kr, rows],
+                    s_rin.at[kr, rows],
+                    s_rout.at[kr, rows],
+                    functools.partial(state_r, kr, q),
+                )
+
         @pl.when(m < NCK)
         def _():
             s_sib[m] = prompt_chunk(1 - s, m)
             state_x(m).start()
             s_own[m] = prompt_chunk(s, m)
 
-        @pl.when(m == 0)
-        def _():
-            carry_x().wait_recv()
-            c_own[...] = c_all[s] + c_rec[...]
-
-        @pl.when(within(m - 1))
-        def _():
-            state_x(m - 1).wait_recv()
-            s_own[m - 1] = s_own[m - 1] + s_rec[m - 1]
-
-        @pl.when(m == i)
-        def _():
-            push_left_sum(c_own, c_lin, c_lout, carry_l)
-
-        @pl.when(m == hr)
-        def _():
-            push_right_sum(c_own, c_rin, c_rout, carry_r)
-
-        kl = m - 1 - i
-
-        @pl.when(within(kl))
-        def _():
-            push_left_sum(
-                s_own.at[kl], s_lin.at[kl], s_lout.at[kl], functools.partial(state_l, kl)
-            )
-
-        kr = m - 1 - hr
-
-        @pl.when(within(kr))
-        def _():
-            push_right_sum(
-                s_own.at[kr], s_rin.at[kr], s_rout.at[kr], functools.partial(state_r, kr)
-            )
-
-        @pl.when(m < NCK)
-        def _():
-            cont_chunk(s, m)
-            cont_chunk(1 - s, m)
-
-        @pl.when(m == far)
+        @pl.when(within(kb))
+        def _():
+            cont_chunk(s, kb)
+            cont_chunk(1 - s, kb)
+
+        @pl.when(kt == -1)
         def _():
             close(c_own, c_lin, c_rin, c_tot, carry_a)
 
-        @pl.when(m == far + 1)
+        @pl.when(kf == -1)
         def _():
             carry_a().wait_recv()
             low = jnp.where(s == 0, c_tot[...], c_ag[...])
@@ -429,8 +459,6 @@
                 seen = jnp.where(inside, part, seen)
             cterm[...] = halves(seen)
 
-        kt = m - 1 - far
-
         @pl.when(within(kt))
         def _():
             close(
@@ -440,18 +468,16 @@
                 s_tot.at[kt],
                 functools.partial(state_a, kt),
             )
-            finish(s, kt, s_tot)
-
-        kf = kt - 1
 
         @pl.when(within(kf))
         def _():
+            finish(s, kf, s_tot)
             state_a(kf).wait_recv()
             finish(1 - s, kf, s_ag)
 
         return unused
 
-    lax.fori_loop(0, NCK + R + 1, step, 0)
+    lax.fori_loop(0, NCK + AHEAD + SKEW * (R - 1) + LAG, step, 0)
 
     ssl[x] = lax.dot_general(
         jnp.ones((8, 128), F32),
@@ -472,11 +498,13 @@
 
         @pl.when(i < R - 1)
         def _():
-            state_l(k).wait_send()
+            state_l(k, 0).wait_send()
+            state_l(k, 1).wait_send()
 
         @pl.when(i > 0)
         def _():
-            state_r(k).wait_send()
+            state_r(k, 0).wait_send()
+            state_r(k, 1).wait_send()
 
         @pl.when(s == 0)
         def _():
@@ -528,21 +556,19 @@
     Gd, N = prompt_b.shape[1:]
     T = cont_x.shape[1]
     NCK = C // 2 // WIDTH
-    picked = lax.broadcasted_iota(jnp.int32, mult_table.shape, 0) == mult_idx[0]
-    multiplier = jnp.sum(jnp.where(picked, mult_table, 0.0))
-    choose = lax.broadcasted_iota(jnp.int32, (steer_vecs.shape[0], 1), 0) == behav_idx[0]
-    vector = jnp.sum(jnp.where(choose, steer_vecs, 0.0), axis=0)
     args = (
         prompt_x,
-        jnp.transpose(prompt_b, (1, 2, 0)),
+        prompt_b,
         prompt_dt,
         cont_x[0],
-        jnp.transpose(cont_bc[0, :, 0], (1, 2, 0)),
-        jnp.transpose(cont_bc[0, :, 1], (1, 0, 2)),
+        cont_bc[0],
         cont_dt[0],
         decay_rate[None],
         skip_gain[None],
-        (multiplier * vector)[None],
+        steer_vecs,
+        mult_table[None],
+        mult_idx,
+        behav_idx,
     )
     vmem, dma = pltpu.VMEM, pltpu.SemaphoreType.DMA
     part = (NCK, N, WIDTH)
@@ -559,8 +585,12 @@
         + [vmem((2,) + carried, F32)]
         + [vmem(carried, F32)] * 8
         + [vmem((N, WIDTH), BF16), vmem((T, 128), F32), vmem((TP, 8, T), F32)]
+        + [vmem((1, C), F32), vmem((Gd, N, tokens), BF16)]
+        + [vmem((Gd, N, T), BF16), vmem((Gd, T, N), BF16)]
         + [dma((2 * R,))] * 2
-        + [dma((NCK + 1,))] * 8
+        + [dma((NCK + 1,))] * 2
+        + [dma((2 * NCK + 1,))] * 4
+        + [dma((NCK + 1,))] * 2
         + [dma((2 * NCK,))] * 2
         + [dma((1,))] * 2
         + [dma((TP,))] * 2
@@ -571,7 +601,8 @@
             jax.ShapeDtypeStruct((T, C), F32),
             jax.ShapeDtypeStruct((8, T), F32),
         ),
-        in_specs=[pl.BlockSpec(memory_space=pltpu.VMEM)] * len(args),
+        in_specs=[pl.BlockSpec(memory_space=pltpu.VMEM)] * (len(args) - 2)
+        + [pl.BlockSpec(memory_space=pltpu.SMEM)] * 2,
         out_specs=(pl.BlockSpec(memory_space=pltpu.VMEM),) * 2,
         scratch_shapes=scratch,
         compiler_params=pltpu.CompilerParams(

time: 113 us -> 83.5 us (0.74)
  Pallas kernels: 99.1 us -> 77.4 us
  local copies, waits for them, and re-layouts: 4.09 us -> 0 us
  other arithmetic: 8.31 us -> 4.69 us
    pallas_call x1, Pallas kernels: 99.1 us -> 77.4 us  [local(): pl.pallas_call(functools.partial(kernel, R, TP, NCK), out_shape=(jax.Shap...]
    unnamed x5 -> x0, local copies, waits for them, and re-layouts: 3.03 us -> none
    reduce_sum x2 -> x0, other arithmetic: 2.37 us -> none  [the longest x1 1.26 us: local(): multiplier = jnp.sum(jnp.where(picked, mult_table, 0.0))]
    mul x1 -> x0, other arithmetic: 1.25 us -> none  [local(): multiplier * vector]
where the time goes in v3:
time: 83.5 us; the launch traced here: 83.3 us
  Pallas kernels  77.4 us (93%)
  other arithmetic  4.69 us (6%)
  between operations  1.31 us (2%)
    pallas_call x1, Pallas kernels, local(): pl.pallas_call(functools.partial(kernel, R, TP, NCK), out_shape=(jax.Shap...  77.4 us
    broadcast_in_dim x1, other arithmetic, local(): (mixed * lax.rsqrt(meansq + 1e-05)[:, None] * norm_gain[None, :]).astype(...  4.01 us

profile of v3, /device:TPU:0, one launch (start us, length us, event | category | flops | bytes accessed | tf_op | source)
XLA Modules:
  0.0 83.3 jit_solution(13038843350070804239)
XLA Ops:
  1.3 77.4 %sweep.1 = (f32[128,8192]{1,0:T(8,128)}, f32[8,128]{1,0:T(8,128)}) custom-call(bf16[64,8192]{1,0:T(8,128)(2,1)} %px.1, bf16[64,4,128]{2,1,0:T(4,128)(2,1)} %pb.1, f32[64,128]{1,0:T(8,128)} %pdt.1, bf16[128,8192]{1,0:T(8,128)(2,1)} %bitcast.10, bf16[128,2,4,128]{3,2,1,0:T(4,128)(2,1)} %bitcast.11, f32[128,128]{1,0:T(8,128)} %bitcast.12, f32[1,128]{1,0:T(1,128)} %bitcast.13, ...), custom_call_target="tpu_custom_call" | custom-call | tf_op jit(solution)/shard_map/sweep/pallas_call | solution.py:598
  78.7 0.7 rsqrt_bitcast_fusion
  79.3 4.0 %fusion = bf16[1,128,8192]{2,1,0:T(8,128)(2,1)} fusion(f32[128,8192]{1,0:T(8,128)} %get-tuple-element.7, f32[8192]{0:T(1024)} %param.21, f32[128]{0:T(128)S(1)} %rsqrt_bitcast_fusion), kind=kLoop, calls=%fused_computation.1 | loop fusion | flops 3145728 | bytes 6324736 | tf_op jit(solution)/shard_map/broadcast_in_dim | solution.py:614

commit v4 on v3

--- a/solution.py
+++ b/solution.py
@@ -56,8 +56,8 @@
     table,
     mult_at,
     behav_at,
+    gain_row,
     out,
-    ss,
     whl,
     colhl,
     rowhl,
@@ -96,6 +96,7 @@
     pbt,
     cbt,
     cc,
+    mix,
     t_send,
     t_recv,
     x_send,
@@ -292,7 +293,7 @@
         scaled = (wide * dot(colhl[...], pick)).astype(BF16)
         inner = dot(gmat[g], scaled)
         gain = dot(skiphl[...], pick)[0:1, :]
-        out[:, slice_at(base)] = dot(rowhl[...], pick) * inner + gain * wide
+        mix[:, slice_at(base)] = dot(rowhl[...], pick) * inner + gain * wide
         row2x[j] = dot(row2hl[...], pick)
 
         @pl.when(s == 0)
@@ -316,8 +317,8 @@
 
         steer = dot(cterm[...], chosen(base // head)) * mv[:, slice_at(base)]
         y = dot(cc[g], incb[...]) + steer
-        mixed = out[:, slice_at(base)] + row2x[j] * y
-        out[:, slice_at(base)] = mixed
+        mixed = mix[:, slice_at(base)] + row2x[j] * y
+        mix[:, slice_at(base)] = mixed
         square = mixed * mixed
         folded = square[:, :128]
         for q in range(1, WIDTH // 128):
@@ -531,7 +532,15 @@
 
     each(2 * R, me, lambda j: tot_copy(j, me).wait_send())
     each(TP, x, lambda j: p_copy(j, j).wait_recv())
-    ss[...] = jnp.sum(ssl[...], axis=0)
+    meansq = jnp.sum(ssl[...], axis=0) / (C * TP)
+    scale = lax.rsqrt(meansq + 1e-05).T[:, 0:1]
+
+    def emit(j, unused):
+        at = pl.ds(pl.multiple_of(j * 512, 512), 512)
+        out[:, at] = (mix[:, at] * scale * gain_row[:, at]).astype(BF16)
+        return unused
+
+    lax.fori_loop(0, C // 512, emit, 0)
     each(TP, x, lambda j: p_copy(j, x).wait_send())
 
 
@@ -569,6 +578,7 @@
         mult_table[None],
         mult_idx,
         behav_idx,
+        norm_gain[None],
     )
     vmem, dma = pltpu.VMEM, pltpu.SemaphoreType.DMA
     part = (NCK, N, WIDTH)
@@ -586,7 +596,7 @@
         + [vmem(carried, F32)] * 8
         + [vmem((N, WIDTH), BF16), vmem((T, 128), F32), vmem((TP, 8, T), F32)]
         + [vmem((1, C), F32), vmem((Gd, N, tokens), BF16)]
-        + [vmem((Gd, N, T), BF16), vmem((Gd, T, N), BF16)]
+        + [vmem((Gd, N, T), BF16), vmem((Gd, T, N), BF16), vmem((T, C), F32)]
         + [dma((2 * R,))] * 2
         + [dma((NCK + 1,))] * 2
         + [dma((2 * NCK + 1,))] * 4
@@ -595,23 +605,20 @@
         + [dma((1,))] * 2
         + [dma((TP,))] * 2
     )
-    mixed, squares = pl.pallas_call(
+    normed = pl.pallas_call(
         functools.partial(kernel, R, TP, NCK),
-        out_shape=(
-            jax.ShapeDtypeStruct((T, C), F32),
-            jax.ShapeDtypeStruct((8, T), F32),
-        ),
-        in_specs=[pl.BlockSpec(memory_space=pltpu.VMEM)] * (len(args) - 2)
-        + [pl.BlockSpec(memory_space=pltpu.SMEM)] * 2,
-        out_specs=(pl.BlockSpec(memory_space=pltpu.VMEM),) * 2,
+        out_shape=jax.ShapeDtypeStruct((T, C), BF16),
+        in_specs=[pl.BlockSpec(memory_space=pltpu.VMEM)] * (len(args) - 3)
+        + [pl.BlockSpec(memory_space=pltpu.SMEM)] * 2
+        + [pl.BlockSpec(memory_space=pltpu.VMEM)],
+        out_specs=pl.BlockSpec(memory_space=pltpu.VMEM),
         scratch_shapes=scratch,
         compiler_params=pltpu.CompilerParams(
             collective_id=0, has_side_effects=True, vmem_limit_bytes=60 * 1024 * 1024
         ),
         name="sweep",
     )(*args)
-    meansq = squares[0] / (norm_gain.shape[0] * TP)
-    return (mixed * lax.rsqrt(meansq + 1e-05)[:, None] * norm_gain[None, :]).astype(BF16)[None]
+    return normed[None]
 
 
 def solution(mesh):

time: 83.5 us -> 82.9 us (level)
  other arithmetic: 4.69 us -> 0 us
  local copies, waits for them, and re-layouts: 0 us -> 3.1 us
  Pallas kernels: 77.4 us -> 78.4 us
    broadcast_in_dim x1 -> x0, other arithmetic: 4.01 us -> none  [local(): (mixed * lax.rsqrt(meansq + 1e-05)[:, None] * norm_gain[None, :]).astype(...]
    unnamed x0 -> x1, local copies, waits for them, and re-layouts: none -> 3.1 us
    pallas_call x1, Pallas kernels: 77.4 us -> 78.4 us  [local(): pl.pallas_call(functools.partial(kernel, R, TP, NCK), out_shape=jax.Shape...]
where the time goes in v4:
time: 82.9 us; the launch traced here: 82.8 us
  Pallas kernels  78.4 us (95%)
  local copies, waits for them, and re-layouts  3.1 us (4%)
  between operations  1.3 us (2%)
    pallas_call x1, Pallas kernels, local(): pl.pallas_call(functools.partial(kernel, R, TP, NCK), out_shape=jax.Shape...  78.4 us
    unnamed x1, local copies, waits for them, and re-layouts  3.1 us

profile of v4, /device:TPU:0, one launch (start us, length us, event | category | flops | bytes accessed | tf_op | source)
XLA Modules:
  0.0 82.8 jit_solution(7534618698044702221)
XLA Ops:
  1.3 78.4 %sweep.1 = bf16[128,8192]{1,0:T(8,128)(2,1)} custom-call(bf16[64,8192]{1,0:T(8,128)(2,1)} %px.1, bf16[64,4,128]{2,1,0:T(4,128)(2,1)} %pb.1, f32[64,128]{1,0:T(8,128)} %pdt.1, bf16[128,8192]{1,0:T(8,128)(2,1)} %bitcast.9, bf16[128,2,4,128]{3,2,1,0:T(4,128)(2,1)} %bitcast.10, f32[128,128]{1,0:T(8,128)} %bitcast.11, f32[1,128]{1,0:T(1,128)} %bitcast.13, ...), custom_call_target="tpu_custom_call" | custom-call | tf_op jit(solution)/shard_map/sweep/pallas_call | solution.py:608
  79.7 3.1 %copy.17 = bf16[1,128,8192]{2,1,0:T(8,128)(2,1)} copy(bf16[1,128,8192]{2,1,0:T(8,128)(2,1)} %bitcast.8) | data formatting | bytes 4194304
